TPU v7x, 128 devices: a whole 4x4x4 slice. The times are simulated.
128 devices in a mesh: slot: 16 (over y, z), head: 2 (over x_lo), conv: 4 (over x_hi, core).
Axes of the slice: x: 4 (x_hi: 2, x_lo: 2; x = x_hi * 2 + x_lo), y: 4, z: 4, core: 2. Of those that a mesh axis runs over, the one named last changes fastest.
Arguments:
- queries: bfloat16 [1024, 64, 128], P(('conv', 'slot'), 'head'), may hold values from -96 to 96
- out_grad: bfloat16 [1024, 64, 128], P(('conv', 'slot'), 'head'), may hold values from -768 to 768
- row_positions: int32 [1024], P('conv'), may hold values from 0 to 8191
- slot_offsets: int32 [16384], P('slot'), may hold values from 0 to 16382, as said below
- cache: float32 [2, 16384, 4, 128], P(None, 'slot', 'head'), may hold values from -12 to 12
- first_moment: float32 [2, 16384, 4, 128], P(None, 'slot', 'head'), may hold values from -6 to 6
- second_moment: float32 [2, 16384, 4, 128], P(None, 'slot', 'head'), may hold values from 0.01 to 1000
Outputs:
- new_cache: float32 [2, 16384, 4, 128], P(None, 'slot', 'head')
- new_first_moment: float32 [2, 16384, 4, 128], P(None, 'slot', 'head')
- new_second_moment: float32 [2, 16384, 4, 128], P(None, 'slot', 'head')
- query_grad: float32 [1024, 64, 128], P(('conv', 'slot'), 'head')
Inputs may be any that keep to these rules, and one draw needn't show every extreme that they name: `slot_offsets`: never falls from one slot to the next; its first two entries are 0.
All inputs are finite; a program needn't handle non-finite values.
Results may differ from a plain program's by a relative error of at most 0.012.
The roundings to bfloat16 on the way count: a program that leaves them out, or rounds other values in their place, can miss the bound.
Values may be sent and summed in bfloat16 or wider, within the bound.
A program may use at most 128 MiB of HBM per device.

v0:
```python
import math
import jax
import jax.numpy as jnp
from jax import lax
from jax.sharding import PartitionSpec as P

STEP = 20
learn_rate = 0.01
beta_one = 0.9
beta_two = 0.95
adam_eps = 1e-08
masked_score = -1e30


def merged(x, axis, combine):
    everything = jax.tree.map(lambda part: lax.all_gather(part, axis), x)
    leading = jax.tree.map(lambda part: part[0], everything)

    def lap(k, so_far):
        return combine(so_far, jax.tree.map(lambda part: part[k], everything))

    return lax.fori_loop(1, lax.axis_size(axis), lap, leading)


def merge_pairs(earlier, later):
    largest = jnp.maximum(earlier[0], later[0])
    return (
        largest,
        earlier[1] * jnp.exp(earlier[0] - largest) + later[1] * jnp.exp(later[0] - largest),
    )


def local(queries, out_grad, row_positions, slot_offsets, cache, first_moment, second_moment):
    query_all, grad_all = (
        lax.all_gather(queries, "slot", axis=0, tiled=True),
        lax.all_gather(out_grad, "slot", axis=0, tiled=True),
    )
    total_rows, head_count, head_width = query_all.shape
    kv_count = cache.shape[2]
    group_heads = head_count // kv_count
    score_scale = 1.0 / math.sqrt(head_width)
    block_rows = min(64, total_rows)
    block_count = total_rows // block_rows
    key_half = cache[0].astype(jnp.bfloat16)
    value_half = cache[1].astype(jnp.bfloat16)
    query_blocks = query_all.reshape(block_count, block_rows, kv_count, group_heads, head_width)
    grad_blocks = grad_all.reshape(block_count, block_rows, kv_count, group_heads, head_width)
    visible_all = (slot_offsets[None, :] <= row_positions[:, None]).reshape(
        block_count, block_rows, -1
    )

    def masked_scores(query_block, visible):
        raw_score = (
            jnp.einsum("rkgd,skd->rkgs", query_block, key_half, preferred_element_type=jnp.float32)
            * score_scale
        )
        return jnp.where(visible[:, None, None, :], raw_score, masked_score)

    def weights_from(scores, visible, offset):
        return jnp.where(visible[:, None, None, :], jnp.exp(scores - offset[..., None]), 0.0)

    def gradient_products(grad_block):
        return jnp.einsum(
            "rkgd,skd->rkgs", grad_block, value_half, preferred_element_type=jnp.float32
        )

    def max_pass(inputs):
        query_block, visible = inputs
        scores = masked_scores(query_block, visible)
        largest = jnp.max(scores, axis=-1)
        return (largest, jnp.sum(weights_from(scores, visible, largest), axis=-1))

    largest, denominator = lax.map(max_pass, (query_blocks, visible_all))
    largest, denominator = merged((largest, denominator), "slot", merge_pairs)
    log_total = largest + jnp.log(denominator)

    def product_pass(inputs):
        query_block, grad_block, visible, block_total = inputs
        probability = weights_from(masked_scores(query_block, visible), visible, block_total)
        return jnp.sum(probability * gradient_products(grad_block), axis=-1)

    partial_sum = lax.map(product_pass, (query_blocks, grad_blocks, visible_all, log_total))
    row_sum = lax.psum(partial_sum, "slot")

    def last_pass(running, inputs):
        key_grad, value_grad = running
        query_block, grad_block, visible, block_total, block_sum = inputs
        probability = weights_from(masked_scores(query_block, visible), visible, block_total)
        prob_grad = gradient_products(grad_block)
        score_grad = (probability * (prob_grad - block_sum[..., None])).astype(jnp.bfloat16)
        prob_half = probability.astype(jnp.bfloat16)
        value_grad = value_grad + jnp.einsum(
            "rkgs,rkgd->skd", prob_half, grad_block, preferred_element_type=jnp.float32
        )
        key_grad = (
            key_grad
            + jnp.einsum(
                "rkgs,rkgd->skd", score_grad, query_block, preferred_element_type=jnp.float32
            )
            * score_scale
        )
        query_part = (
            jnp.einsum("rkgs,skd->rkgd", score_grad, key_half, preferred_element_type=jnp.float32)
            * score_scale
        )
        return ((key_grad, value_grad), query_part)

    empty_grad = jnp.zeros(key_half.shape, jnp.float32)
    (key_grad, value_grad), query_parts = lax.scan(
        last_pass,
        (empty_grad, empty_grad),
        (query_blocks, grad_blocks, visible_all, log_total, row_sum),
    )
    query_terms = query_parts.reshape(total_rows, head_count, head_width)
    summed = lax.psum(query_terms, "slot")
    own_rows = queries.shape[0]
    query_grad = lax.dynamic_slice_in_dim(summed, lax.axis_index("slot") * own_rows, own_rows, 0)
    key_total, value_total = lax.psum((key_grad, value_grad), "conv")
    slot_grad = jnp.stack([key_total, value_total])
    new_first = beta_one * first_moment + (1.0 - beta_one) * slot_grad
    new_second = beta_two * second_moment + (1.0 - beta_two) * slot_grad * slot_grad
    first_fix = 1.0 - beta_one**STEP
    second_fix = 1.0 - beta_two**STEP
    new_cache = cache - learn_rate * (new_first / first_fix) / (
        jnp.sqrt(new_second / second_fix) + adam_eps
    )
    return (new_cache, new_first, new_second, query_grad)


def solution(mesh):
    in_specs = (
        P(("conv", "slot"), "head", None),
        P(("conv", "slot"), "head", None),
        P("conv"),
        P("slot"),
        P(None, "slot", "head", None),
        P(None, "slot", "head", None),
        P(None, "slot", "head", None),
    )
    out_specs = (
        P(None, "slot", "head", None),
        P(None, "slot", "head", None),
        P(None, "slot", "head", None),
        P(("conv", "slot"), "head", None),
    )
    return jax.shard_map(local, mesh=mesh, in_specs=in_specs, out_specs=out_specs, check_vma=False)
```

profile of v0, /device:TPU:1, one launch (start us, length us, event | category | flops | bytes accessed | tf_op | source)
XLA Modules:
  0.0 525.3 jit_solution(10511550598650439508)
XLA Ops:
  9.5 1.8 copy.70
  13.1 43.8 %all-gather.5.cloned.1.call-done = bf16[256,32,128]{2,1,0:T(8,128)(2,1)} async-done(((bf16[16,32,128]{2,1,0:T(8,128)(2,1)}), bf16[256,32,128]{2,1,0:T(8,128)(2,1)}) %all-gather.5.cloned.1.call-update) | async-done | bytes 2097168 | tf_op jit(solution)/shard_map/all_gather | solution.py:35
  56.9 3.3 copy.50
  60.1 43.2 %all-gather.7.cloned.1.call-done = bf16[256,32,128]{2,1,0:T(8,128)(2,1)} async-done(((bf16[16,32,128]{2,1,0:T(8,128)(2,1)}), bf16[256,32,128]{2,1,0:T(8,128)(2,1)}) %all-gather.7.cloned.1.call-update) | async-done | bytes 2097168 | tf_op jit(solution)/shard_map/all_gather | solution.py:36
  103.3 3.3 copy.51
  106.6 23.2 %while.54 = (s32[]{:T(128)}, f32[4,64,2,16]{1,3,2,0:T(8,128)S(1)}, f32[4,64,2,16]{1,3,2,0:T(8,128)S(1)}, pred[4,64,1024]{2,1,0:T(8,128)(4,1)S(1)}, bf16[4,64,2,1...) while((s32[]{:T(128)}, f32[4,64,2,16]{1,3,2,0:T(8,128)S(1)}, ...), condition=%wide.region_3.4_spmd, body=%wide.region_0.3_spmd.sunk | while | flops 553644032 | bytes 18210912 | solution.py:73
  106.6 2.8 bitcast_reduce_fusion.2
  109.4 2.8 fusion.87
  112.4 2.8 bitcast_reduce_fusion.2
  115.2 2.8 fusion.87
  118.2 2.8 bitcast_reduce_fusion.2
  121.0 2.8 fusion.87
  124.0 2.8 bitcast_reduce_fusion.2
  126.8 2.8 fusion.87
  129.8 19.1 %all-gather.1 = f32[64,64,2,16]{1,3,2,0:T(8,128)S(1)} all-gather(f32[4,64,2,16]{1,3,2,0:T(8,128)S(1)} %get-tuple-element.272), channel_id=3, replica_groups=mesh['slot'=16,'head'=2,'conv'=4] {'slot'}, dimensions={0}, use_global_device_ids=true | all-gather | bytes 557056 | tf_op jit(solution)/shard_map/all_gather | solution.py:16
  148.9 17.4 %all-gather = f32[64,64,2,16]{1,3,2,0:T(8,128)S(1)} all-gather(f32[4,64,2,16]{1,3,2,0:T(8,128)S(1)} %get-tuple-element.271), channel_id=2, replica_groups=mesh['slot'=16,'head'=2,'conv'=4] {'slot'}, dimensions={0}, use_global_device_ids=true | all-gather | bytes 557056 | tf_op jit(solution)/shard_map/all_gather | solution.py:16
  166.3 1.0 copy-done.4
  167.2 13.9 %while.55 = (s32[]{:T(128)}, f32[4,64,2,16]{1,3,2,0:T(8,128)S(1)}, f32[4,64,2,16]{1,3,2,0:T(8,128)S(1)}, f32[16,4,64,2,16]{2,4,3,1,0:T(8,128)}, f32[16,4,64,2,16...) while((s32[]{:T(128)}, f32[4,64,2,16]{1,3,2,0:T(8,128)S(1)}, f32[4,64,2,16]{1,3,2,0:T(8,128)S(1)}, ...), condition=%wide.region_5.6_spmd, body=%wide.region_4.5_spmd.sunk | while | flops 49157 | bytes 196731 | solution.py:22
  168.1 0.9 fusion.88
  169.1 0.9 fusion.88
  170.0 0.9 fusion.88
  181.5 31.2 %while.56 = (s32[]{:T(128)}, f32[4,64,2,16]{3,1,2,0:T(8,128)}, pred[4,64,1024]{2,1,0:T(8,128)(4,1)S(1)}, bf16[4,64,2,16,128]{4,3,1,2,0:T(8,128)(2,1)}, bf16[1024...) while((s32[]{:T(128)}, f32[4,64,2,16]{3,1,2,0:T(8,128)}, ...), condition=%wide.region_8.9_spmd, body=%wide.region_6.8_spmd.sunk | while | flops 1086322688 | bytes 21397652 | solution.py:82
  181.5 2.4 fusion.93
  183.9 4.7 fusion.94
  189.4 2.4 fusion.93
  191.7 4.7 fusion.94
  197.1 2.4 fusion.93
  199.5 4.7 fusion.94
  204.9 2.4 fusion.93
  207.3 4.7 fusion.94
  212.7 61.1 %psum.28 = f32[4,64,2,16]{3,1,2,0:T(8,128)S(1)} all-reduce(f32[4,64,2,16]{3,1,2,0:T(8,128)} %get-tuple-element.275), channel_id=1, replica_groups=mesh['slot'=16,'head'=2,'conv'=4] {'slot'}, use_global_device_ids=true, to_apply=%region_9.10 | all-reduce | flops 8192 | bytes 65536 | tf_op jit(solution)/shard_map/psum | solution.py:83
  273.8 52.7 %while.57 = (s32[]{:T(128)}, f32[1024,2,128]{0,2,1:T(8,128)S(1)}, f32[1024,2,128]{0,2,1:T(8,128)S(1)}, f32[4,64,2,16,128]{4,3,2,1,0:T(8,128)}, bf16[4,64,2,16,12...) while((s32[]{:T(128)}, f32[1024,2,128]{0,2,1:T(8,128)S(1)}, ...), condition=%wide.region_11.12_spmd.clone, body=%wide.region_10.11_spmd.clone.sunk | while | flops 2711093248 | bytes 59867360 | solution.py:109
  273.9 2.4 fusion.105
  276.4 2.7 fusion.108
  279.1 3.5 fusion.106
  282.5 2.1 fusion.107
  284.7 1.2 fusion.109
  285.9 1.1 copy_dynamic-update-slice_fusion.2
  287.1 2.4 fusion.105
  289.6 2.7 fusion.108
  292.2 3.5 fusion.106
  295.7 2.1 fusion.107
  297.8 1.2 fusion.109
  299.1 1.2 copy_dynamic-update-slice_fusion.2
  300.3 2.4 fusion.105
  302.7 2.7 fusion.108
  305.4 3.5 fusion.106
  308.9 2.1 fusion.107
  311.0 1.2 fusion.109
  312.3 1.1 copy_dynamic-update-slice_fusion.2
  313.4 2.4 fusion.105
  315.9 2.7 fusion.108
  318.6 3.5 fusion.106
  322.1 2.1 fusion.107
  324.2 1.2 fusion.109
  325.4 1.1 copy_dynamic-update-slice_fusion.2
  326.6 1.3 copy.52
  327.9 1.3 copy.53
  329.7 81.8 %all-reduce.6.cloned.1.call-done = (f32[1,1024,2,128]{3,2,1,0:T(2,128)}, f32[1,1024,2,128]{3,2,1,0:T(2,128)}) async-done(((f32[1,1024,2,128]{3,2,1,0:T(2,128)}, f32[1,1024,2,128]{3,2,1,0:T(2,128)}), (f32[1,1024,2,128]{3,2,1,0:T(2,128)}, f32[1,1024,2,128]{3,2,1,0:T(2,128)})) %all-reduce.6.cloned.1.call-update) | async-done | bytes 2097168 | tf_op jit(solution)/shard_map/psum | solution.py:118
  411.5 1.4 constant_dynamic-update-slice_fusion.3
  413.0 1.5 constant_dynamic-update-slice_fusion.2
  414.5 8.0 %divide_subtract_fusion = (f32[2,1024,2,128]{3,2,1,0:T(2,128)}, f32[2,1024,2,128]{3,2,1,0:T(2,128)}, f32[2,1024,2,128]{3,2,1,0:T(2,128)}) fusion(f32[2,1024,2,128]{3,2,1,0:T(2,128)S(1)} %copy-done, f32[2,1024,2,128]{3,2,1,0:T(2,128)S(1)} %constant_dynamic-update-slice_fusion.2, f32[2,1024,2,128]{3,2,1,0:T(2,128)S(1)} %copy-done.1, ...), kind=kLoop, calls=%fused_computation.80 | loop fusion | flops 6291456 | bytes 14680064 | tf_op jit(solution)/shard_map/sub | solution.py:124
  422.5 94.6 %all-reduce.4.cloned.1.call-done = f32[256,32,128]{2,1,0:T(8,128)} async-done(((f32[256,32,128]{2,1,0:T(8,128)}), f32[256,32,128]{2,1,0:T(8,128)}) %all-reduce.4.cloned.1.call-update) | async-done | bytes 4194320 | tf_op jit(solution)/shard_map/psum | solution.py:115
  517.1 1.7 constant_dynamic-slice_fusion
  (103 shorter events, 19.2 us)
Async XLA Ops:
  7.2 49.7 %all-gather.5.cloned.1.call-start = ((), (), s32[]{:S(2)}) async-start(), calls=%async_computation | async-start | bytes 2228224 | tf_op jit(solution)/shard_map/all_gather | solution.py:35
  7.9 95.4 %all-gather.7.cloned.1.call-start = ((), (), s32[]{:S(2)}) async-start(), calls=%async_computation.1 | async-start | bytes 2228224 | tf_op jit(solution)/shard_map/all_gather | solution.py:36
  8.6 402.9 %all-reduce.6.cloned.1.call-start = ((), (), s32[]{:S(2)}) async-start(), calls=%async_computation.3 | async-start | bytes 4194304 | tf_op jit(solution)/shard_map/psum | solution.py:118
  166.2 1.0 copy-start.4
  181.4 92.4 %copy-start.5 = (f32[1024,2,128]{0,2,1:T(8,128)S(1)}, f32[1024,2,128]{0,2,1:T(8,128)}, u32[]{:S(2)}) copy-start(f32[1024,2,128]{0,2,1:T(8,128)} %custom-call.1) | copy-start | bytes 3145732
  181.5 2.4 copy-start.6
  189.3 2.4 copy-start.6
  197.1 2.4 copy-start.6
  204.9 2.4 copy-start.6
  273.9 2.5 copy-start.3
  276.4 2.7 copy-start.7
  287.1 2.5 copy-start.3
  289.5 2.7 copy-start.7
  300.3 2.5 copy-start.3
  302.7 2.7 copy-start.7
  313.4 2.5 copy-start.3
  315.9 2.7 copy-start.7
  329.2 187.9 %all-reduce.4.cloned.1.call-start = ((), (), s32[]{:S(2)}) async-start(), calls=%async_computation.2 | async-start | bytes 8388608 | tf_op jit(solution)/shard_map/psum | solution.py:115
  329.2 85.2 %copy-start = (f32[2,1024,2,128]{3,2,1,0:T(2,128)S(1)}, f32[2,1024,2,128]{3,2,1,0:T(2,128)}, u32[]{:S(2)}) copy-start(f32[2,1024,2,128]{3,2,1,0:T(2,128)} %param.19) | copy-start | bytes 6291460
  411.5 3.0 copy-start.1
  411.5 3.0 copy-start.2
Sparse Core Ops, SparseCore 0:
  10.1 46.6 all-gather.4
  59.0 44.2 all-gather.6
  329.3 82.1 all-reduce.5
  414.7 102.2 all-reduce.3
where the time goes:
time: 527 us; the launch traced here: 525 us
  waiting for transfers between devices  265 us (50%)
  blocking collectives  97.6 us (19%)
  matrix products  87.3 us (17%)
  other arithmetic  33.9 us (6%)
  local copies, waits for them, and re-layouts  26.4 us (5%)
  between operations  13.9 us (3%)
    psum x1, waiting for transfers between devices, local(): summed = lax.psum(query_terms, 'slot')  94.6 us
    psum x1, waiting for transfers between devices, local(): key_total, value_total = lax.psum((key_grad, value_grad), 'conv')  81.8 us
    psum x1, blocking collectives, local(): row_sum = lax.psum(partial_sum, 'slot')  61.1 us
    all_gather x1, waiting for transfers between devices, local(): lax.all_gather(queries, 'slot', axis=0, tiled=True)  43.8 us
    all_gather x1, waiting for transfers between devices, local(): lax.all_gather(out_grad, 'slot', axis=0, tiled=True)  43.2 us
    all_gather x2, blocking collectives, merged(): everything = jax.tree.map(lambda part: lax.all_gather(part, axis), x)  36.5 us
    dot_general x8, matrix products, gradient_products(): jnp.einsum('rkgd,skd->rkgs', grad_block, value_half, preferred_element_ty...  32.8 us
    dot_general x12, matrix products, masked_scores(): jnp.einsum('rkgd,skd->rkgs', query_block, key_half, preferred_element_typ...  30.3 us
  transfers between devices with their start and end apart: 4, of which 4 were waited for; matrix products, arithmetic and copies ran while one was open for 4% of the time, Pallas kernels for 0%

commit v1 on v0

--- a/solution.py
+++ b/solution.py
@@ -32,7 +32,9 @@
 
 def local(queries, out_grad, row_positions, slot_offsets, cache, first_moment, second_moment):
     query_all, grad_all = (
-        lax.all_gather(queries, "slot", axis=0, tiled=True),
+        jnp.concatenate(
+            lax.all_to_all(jnp.stack([queries] * lax.axis_size("slot")), "slot", 0, 0), axis=0
+        ),
         lax.all_gather(out_grad, "slot", axis=0, tiled=True),
     )
     total_rows, head_count, head_width = query_all.shape

time: 527 us -> 476 us (0.903)
  waiting for transfers between devices: 265 us -> 203 us
  starting transfers between devices: 0.16 us -> 8.89 us
    all_gather x1 -> x0, waiting for transfers between devices: 43.8 us -> none  [local(): lax.all_gather(queries, 'slot', axis=0, tiled=True)]
    all_gather x1, waiting for transfers between devices: 43.2 us -> 0.02 us  [local(): lax.all_gather(out_grad, 'slot', axis=0, tiled=True)]
    all_to_all x0 -> x1, waiting for transfers between devices: none -> 25.4 us  [local(): lax.all_to_all(jnp.stack([queries] * lax.axis_size('slot')), 'slot', 0, 0)]
    all_to_all x0 -> x1, starting transfers between devices: none -> 8.77 us  [local(): lax.all_to_all(jnp.stack([queries] * lax.axis_size('slot')), 'slot', 0, 0)]
    unnamed x14 -> x12, local copies, waits for them, and re-layouts: 10.8 us -> 10.6 us
  transfers between devices with their start and end apart: 4 -> 4, of which waited for: 4 -> 3; matrix products, arithmetic and copies ran while one was open for 4% -> 12% of each run, Pallas kernels for 0% -> 0%
where the time goes in v1:
time: 476 us; the launch traced here: 474 us
  waiting for transfers between devices  203 us (43%)
  blocking collectives  97.5 us (20%)
  matrix products  87.3 us (18%)
  other arithmetic  35.1 us (7%)
  local copies, waits for them, and re-layouts  28.1 us (6%)
  between operations  13.9 us (3%)
  starting transfers between devices  8.89 us (2%)
    psum x1, waiting for transfers between devices, local(): summed = lax.psum(query_terms, 'slot')  93.3 us
    psum x1, waiting for transfers between devices, local(): key_total, value_total = lax.psum((key_grad, value_grad), 'conv')  82.7 us
    psum x1, blocking collectives, local(): row_sum = lax.psum(partial_sum, 'slot')  61.4 us
    all_gather x2, blocking collectives, merged(): everything = jax.tree.map(lambda part: lax.all_gather(part, axis), x)  36.1 us
    dot_general x8, matrix products, gradient_products(): jnp.einsum('rkgd,skd->rkgs', grad_block, value_half, preferred_element_ty...  32.8 us
    dot_general x12, matrix products, masked_scores(): jnp.einsum('rkgd,skd->rkgs', query_block, key_half, preferred_element_typ...  30.3 us
    all_to_all x1, waiting for transfers between devices, local(): lax.all_to_all(jnp.stack([queries] * lax.axis_size('slot')), 'slot', 0, 0)  25.4 us
    add x15, other arithmetic, merge_pairs(): earlier[1] * jnp.exp(earlier[0] - largest)  13.6 us
  transfers between devices with their start and end apart: 4, of which 3 were waited for; matrix products, arithmetic and copies ran while one was open for 12% of the time, Pallas kernels for 0%

profile of v1, /device:TPU:1, one launch (start us, length us, event | category | flops | bytes accessed | tf_op | source)
XLA Modules:
  0.0 474.1 jit_solution(197604858819548774)
XLA Ops:
  7.2 2.6 stack.8
  9.8 8.8 %all-to-all-start = ((bf16[16,16,32,128]{3,2,1,0:T(8,128)(2,1)}), bf16[16,16,32,128]{3,2,1,0:T(8,128)(2,1)}, u32[]{:S(2)}, u32[]{:S(2)}) async-start(bf16[16,16,32,128]{3,2,1,0:T(8,128)(2,1)} %stack.8), calls=%async_computation | async-start | bytes 4194304 | tf_op jit(solution)/shard_map/all_to_all | solution.py:36
  19.5 1.8 copy.70
  22.4 25.4 %all-to-all-done = bf16[16,16,32,128]{3,2,1,0:T(8,128)(2,1)} async-done(((bf16[16,16,32,128]{3,2,1,0:T(8,128)(2,1)}), bf16[16,16,32,128]{3,2,1,0:T(8,128)(2,1)}, u32[]{:S(2)}, u32[]{:S(2)}) %all-to-all-start) | async-done | bytes 2097184 | tf_op jit(solution)/shard_map/all_to_all | solution.py:36
  47.8 3.3 copy.50
  51.1 23.2 %while.54 = (s32[]{:T(128)}, f32[4,64,2,16]{1,3,2,0:T(8,128)S(1)}, f32[4,64,2,16]{1,3,2,0:T(8,128)S(1)}, pred[4,64,1024]{2,1,0:T(8,128)(4,1)S(1)}, bf16[4,64,2,1...) while((s32[]{:T(128)}, f32[4,64,2,16]{1,3,2,0:T(8,128)S(1)}, ...), condition=%wide.region_3.4_spmd, body=%wide.region_0.3_spmd.sunk | while | flops 553644032 | bytes 18210912 | solution.py:75
  51.1 2.8 bitcast_reduce_fusion.2
  53.8 2.8 fusion.87
  56.9 2.8 bitcast_reduce_fusion.2
  59.6 2.8 fusion.87
  62.7 2.8 bitcast_reduce_fusion.2
  65.4 2.8 fusion.87
  68.4 2.8 bitcast_reduce_fusion.2
  71.2 2.8 fusion.87
  74.2 17.3 %all-gather.1 = f32[64,64,2,16]{1,3,2,0:T(8,128)S(1)} all-gather(f32[4,64,2,16]{1,3,2,0:T(8,128)S(1)} %get-tuple-element.272), channel_id=3, replica_groups=mesh['slot'=16,'head'=2,'conv'=4] {'slot'}, dimensions={0}, use_global_device_ids=true | all-gather | bytes 557056 | tf_op jit(solution)/shard_map/all_gather | solution.py:16
  91.5 18.8 %all-gather = f32[64,64,2,16]{1,3,2,0:T(8,128)S(1)} all-gather(f32[4,64,2,16]{1,3,2,0:T(8,128)S(1)} %get-tuple-element.271), channel_id=2, replica_groups=mesh['slot'=16,'head'=2,'conv'=4] {'slot'}, dimensions={0}, use_global_device_ids=true | all-gather | bytes 557056 | tf_op jit(solution)/shard_map/all_gather | solution.py:16
  110.4 1.0 copy-done.1
  111.3 13.9 %while.55 = (s32[]{:T(128)}, f32[4,64,2,16]{1,3,2,0:T(8,128)S(1)}, f32[4,64,2,16]{1,3,2,0:T(8,128)S(1)}, f32[16,4,64,2,16]{2,4,3,1,0:T(8,128)}, f32[16,4,64,2,16...) while((s32[]{:T(128)}, f32[4,64,2,16]{1,3,2,0:T(8,128)S(1)}, f32[4,64,2,16]{1,3,2,0:T(8,128)S(1)}, ...), condition=%wide.region_5.6_spmd, body=%wide.region_4.5_spmd.sunk | while | flops 49157 | bytes 196731 | solution.py:22
  112.3 0.9 fusion.88
  123.4 0.9 fusion.88
  125.6 3.3 copy.51
  128.9 31.2 %while.56 = (s32[]{:T(128)}, f32[4,64,2,16]{3,1,2,0:T(8,128)}, pred[4,64,1024]{2,1,0:T(8,128)(4,1)S(1)}, bf16[4,64,2,16,128]{4,3,1,2,0:T(8,128)(2,1)}, bf16[1024...) while((s32[]{:T(128)}, f32[4,64,2,16]{3,1,2,0:T(8,128)}, ...), condition=%wide.region_8.9_spmd, body=%wide.region_6.8_spmd.sunk | while | flops 1086322688 | bytes 21397652 | solution.py:84
  128.9 2.4 fusion.93
  131.4 4.7 %fusion.94 = f32[64,2,16]{2,0,1:T(8,128)S(1)} fusion(f32[2,64,16,1024]{3,2,1,0:T(8,128)S(1)} %fusion.93, f32[64,2,16]{2,0,1:T(8,128)S(1)} %dynamic-slice_bitcast_fusion.12, pred[64,1024]{1,0:T(8,128)(4,1)S(1)} %dynamic-slice_bitcast_fusion.13, bf16[1024,2,128]{2,0,1:T(8,128)(2,1)S(1)} %copy-done.3, ...), kind=kOutput, calls=%fused_computation.20.clone.1 | convolution fusion | flops 549451776 | bytes 9641988 | tf_op jit(solution)/shard_map/while/body/eval_jaxpr/rkgd,skd->rkgs/dot_general | solution.py:65
  136.8 2.4 fusion.93
  139.2 4.7 %fusion.94 = f32[64,2,16]{2,0,1:T(8,128)S(1)} fusion(f32[2,64,16,1024]{3,2,1,0:T(8,128)S(1)} %fusion.93, f32[64,2,16]{2,0,1:T(8,128)S(1)} %dynamic-slice_bitcast_fusion.12, pred[64,1024]{1,0:T(8,128)(4,1)S(1)} %dynamic-slice_bitcast_fusion.13, bf16[1024,2,128]{2,0,1:T(8,128)(2,1)S(1)} %copy-done.3, ...), kind=kOutput, calls=%fused_computation.20.clone.1 | convolution fusion | flops 549451776 | bytes 9641988 | tf_op jit(solution)/shard_map/while/body/eval_jaxpr/rkgd,skd->rkgs/dot_general | solution.py:65
  144.6 2.4 fusion.93
  146.9 4.7 %fusion.94 = f32[64,2,16]{2,0,1:T(8,128)S(1)} fusion(f32[2,64,16,1024]{3,2,1,0:T(8,128)S(1)} %fusion.93, f32[64,2,16]{2,0,1:T(8,128)S(1)} %dynamic-slice_bitcast_fusion.12, pred[64,1024]{1,0:T(8,128)(4,1)S(1)} %dynamic-slice_bitcast_fusion.13, bf16[1024,2,128]{2,0,1:T(8,128)(2,1)S(1)} %copy-done.3, ...), kind=kOutput, calls=%fused_computation.20.clone.1 | convolution fusion | flops 549451776 | bytes 9641988 | tf_op jit(solution)/shard_map/while/body/eval_jaxpr/rkgd,skd->rkgs/dot_general | solution.py:65
  152.4 2.4 fusion.93
  154.7 4.7 %fusion.94 = f32[64,2,16]{2,0,1:T(8,128)S(1)} fusion(f32[2,64,16,1024]{3,2,1,0:T(8,128)S(1)} %fusion.93, f32[64,2,16]{2,0,1:T(8,128)S(1)} %dynamic-slice_bitcast_fusion.12, pred[64,1024]{1,0:T(8,128)(4,1)S(1)} %dynamic-slice_bitcast_fusion.13, bf16[1024,2,128]{2,0,1:T(8,128)(2,1)S(1)} %copy-done.3, ...), kind=kOutput, calls=%fused_computation.20.clone.1 | convolution fusion | flops 549451776 | bytes 9641988 | tf_op jit(solution)/shard_map/while/body/eval_jaxpr/rkgd,skd->rkgs/dot_general | solution.py:65
  160.1 61.4 %psum.28 = f32[4,64,2,16]{3,1,2,0:T(8,128)S(1)} all-reduce(f32[4,64,2,16]{3,1,2,0:T(8,128)} %get-tuple-element.275), channel_id=1, replica_groups=mesh['slot'=16,'head'=2,'conv'=4] {'slot'}, use_global_device_ids=true, to_apply=%region_9.10 | all-reduce | flops 8192 | bytes 65536 | tf_op jit(solution)/shard_map/psum | solution.py:85
  221.5 52.7 %while.57 = (s32[]{:T(128)}, f32[1024,2,128]{0,2,1:T(8,128)S(1)}, f32[1024,2,128]{0,2,1:T(8,128)S(1)}, f32[4,64,2,16,128]{4,3,2,1,0:T(8,128)}, bf16[4,64,2,16,12...) while((s32[]{:T(128)}, f32[1024,2,128]{0,2,1:T(8,128)S(1)}, ...), condition=%wide.region_11.12_spmd.clone, body=%wide.region_10.11_spmd.clone.sunk | while | flops 2711093248 | bytes 59867360 | solution.py:111
  221.6 2.4 fusion.105
  224.0 2.7 fusion.108
  226.7 3.5 fusion.106
  230.2 2.1 fusion.107
  232.3 1.2 fusion.109
  233.6 1.1 copy_dynamic-update-slice_fusion.2
  234.7 2.4 fusion.105
  237.2 2.7 fusion.108
  239.9 3.5 fusion.106
  243.4 2.1 fusion.107
  245.5 1.2 fusion.109
  246.7 1.2 copy_dynamic-update-slice_fusion.2
  247.9 2.4 fusion.105
  250.4 2.7 fusion.108
  253.1 3.5 fusion.106
  256.6 2.1 fusion.107
  258.7 1.2 fusion.109
  259.9 1.1 copy_dynamic-update-slice_fusion.2
  261.1 2.4 fusion.105
  263.6 2.7 fusion.108
  266.3 3.5 fusion.106
  269.7 2.1 fusion.107
  271.8 1.2 fusion.109
  273.1 1.2 copy_dynamic-update-slice_fusion.2
  274.2 1.3 copy.52
  275.5 1.3 copy.53
  277.6 82.7 %all-reduce.6.cloned.1.call-done = (f32[1,1024,2,128]{3,2,1,0:T(2,128)}, f32[1,1024,2,128]{3,2,1,0:T(2,128)}) async-done(((f32[1,1024,2,128]{3,2,1,0:T(2,128)}, f32[1,1024,2,128]{3,2,1,0:T(2,128)}), (f32[1,1024,2,128]{3,2,1,0:T(2,128)}, f32[1,1024,2,128]{3,2,1,0:T(2,128)})) %all-reduce.6.cloned.1.call-update) | async-done | bytes 2097168 | tf_op jit(solution)/shard_map/psum | solution.py:120
  360.2 1.3 constant_dynamic-update-slice_fusion.3
  361.5 1.4 constant_dynamic-update-slice_fusion.2
  362.9 9.8 %divide_subtract_fusion = (f32[2,1024,2,128]{3,2,1,0:T(2,128)}, f32[2,1024,2,128]{3,2,1,0:T(2,128)}, f32[2,1024,2,128]{3,2,1,0:T(2,128)}) fusion(f32[2,1024,2,128]{3,2,1,0:T(2,128)} %param.19, f32[2,1024,2,128]{3,2,1,0:T(2,128)S(1)} %constant_dynamic-update-slice_fusion.2, f32[2,1024,2,128]{3,2,1,0:T(2,128)} %param.20, f32[2,1024,2,128]{3,2,1,0:T(2,128)} %param.21), kind=kLoop, calls=%fused_computation.80 | loop fusion | flops 6291456 | bytes 14680064 | tf_op jit(solution)/shard_map/sub | solution.py:126
  372.7 93.3 %all-reduce.4.cloned.1.call-done = f32[256,32,128]{2,1,0:T(8,128)} async-done(((f32[256,32,128]{2,1,0:T(8,128)}), f32[256,32,128]{2,1,0:T(8,128)}) %all-reduce.4.cloned.1.call-update) | async-done | bytes 4194320 | tf_op jit(solution)/shard_map/psum | solution.py:117
  465.9 1.7 constant_dynamic-slice_fusion
  (101 shorter events, 18.2 us)
Async XLA Ops:
  7.2 12.3 %copy-start.6 = (s32[256]{0:T(256)S(1)}, s32[256]{0:T(256)}, u32[]{:S(2)}) copy-start(s32[256]{0:T(256)} %param.17) | copy-start | bytes 3076
  9.8 11.5 %copy-start.5 = (s32[1024]{0:T(1024)S(1)}, s32[1024]{0:T(1024)}, u32[]{:S(2)}) copy-start(s32[1024]{0:T(1024)} %param.18) | copy-start | bytes 12292
  9.8 38.0 %all-to-all-start = ((bf16[16,16,32,128]{3,2,1,0:T(8,128)(2,1)}), bf16[16,16,32,128]{3,2,1,0:T(8,128)(2,1)}, u32[]{:S(2)}, u32[]{:S(2)}) async-start(bf16[16,16,32,128]{3,2,1,0:T(8,128)(2,1)} %stack.8), calls=%async_computation | async-start | bytes 4194304 | tf_op jit(solution)/shard_map/all_to_all | solution.py:36
  18.6 107.0 %all-gather.4.cloned.1.call-start = ((), (), s32[]{:S(2)}) async-start(), calls=%async_computation.1 | async-start | bytes 2228224 | tf_op jit(solution)/shard_map/all_gather | solution.py:38
  19.3 340.9 %all-reduce.6.cloned.1.call-start = ((), (), s32[]{:S(2)}) async-start(), calls=%async_computation.3 | async-start | bytes 4194304 | tf_op jit(solution)/shard_map/psum | solution.py:120
  110.4 1.0 copy-start.1
  128.9 92.6 %copy-start.2 = (f32[1024,2,128]{0,2,1:T(8,128)S(1)}, f32[1024,2,128]{0,2,1:T(8,128)}, u32[]{:S(2)}) copy-start(f32[1024,2,128]{0,2,1:T(8,128)} %custom-call.1) | copy-start | bytes 3145732
  128.9 2.4 copy-start.3
  136.8 2.4 copy-start.3
  144.6 2.4 copy-start.3
  152.3 2.4 copy-start.3
  221.6 2.5 copy-start
  224.0 2.7 copy-start.4
  234.7 2.5 copy-start
  237.2 2.7 copy-start.4
  247.9 2.5 copy-start
  250.4 2.7 copy-start.4
  261.1 2.5 copy-start
  263.6 2.7 copy-start.4
  276.8 189.1 %all-reduce.4.cloned.1.call-start = ((), (), s32[]{:S(2)}) async-start(), calls=%async_computation.2 | async-start | bytes 8388608 | tf_op jit(solution)/shard_map/psum | solution.py:117
Sparse Core Ops, SparseCore 0:
  21.5 52.4 all-gather.3
  277.0 83.2 all-reduce.5
  363.6 102.2 all-reduce.3
